TPU v7x, 512 devices: a whole 4x8x8 slice. The times are simulated.
512 devices in a mesh: pipe: 8 (over y_hi, core), ctx: 16 (over z, y_lo), dp: 4 (over x).
Axes of the slice: x: 4, y: 8 (y_hi: 4, y_lo: 2; y = y_hi * 2 + y_lo), z: 8, core: 2. Of those that a mesh axis runs over, the one named last changes fastest.
Arguments:
- state: bfloat16 [8, 4, 2048, 1024], P('pipe', 'dp', 'ctx'), may hold values from -36 to 36
- weights: bfloat16 [2, 8, 1024, 256], P(None, 'pipe'), may hold values from -0.1875 to 0.1875
- out_grad: bfloat16 [2, 8, 4, 2048, 1024], P(None, 'pipe', 'dp', 'ctx'), may hold values from -0.59765625 to 0.59765625
- start_span: int32 [8, 4], P(None, 'dp'), may hold values from 0 to 1
- block_order: int32 [32], replicated, may hold values from 0 to 31, each once
Outputs:
- state_out: bfloat16 [8, 4, 2048, 1024], P('pipe', 'dp', 'ctx')
- weight_grads: float32 [2, 8, 1024, 256], P(None, 'pipe')
All inputs are finite; a program needn't handle non-finite values.
Results may differ from a plain program's by a relative error of at most 0.012.
Values may be sent and summed in bfloat16 or wider, within the bound.
No kernel may reach another device: no remote copies, remote signals or barrier semaphores. Data moves between devices by JAX's collectives and lax.ppermute only.
A program may use at most 64 MiB of HBM per device.

v0:
```python
import math
import jax
import jax.numpy as jnp
from jax import lax
from jax.sharding import PartitionSpec as P

EPS = 1e-05


def from_behind(block, axis, distance):
    devices = range(lax.axis_size(axis))
    route = [((i - distance) % len(devices), i) for i in devices]
    return lax.ppermute(block, axis, route)


def rms_scale(values):
    return lax.rsqrt(jnp.mean(values * values, axis=-1, keepdims=True) + EPS)


def token_positions(block_order, seq_total):
    half_count = block_order.shape[0]
    half_len = seq_total // half_count
    row_ids = jnp.arange(seq_total, dtype=jnp.int32)
    selected = (row_ids // half_len)[:, None] == jnp.arange(half_count, dtype=jnp.int32)[None, :]
    block_ids = jnp.sum(jnp.where(selected, block_order[None, :], 0), axis=1)
    return block_ids * half_len + row_ids % half_len


def shards(state, weights, out_grad, start_span, block_order):
    tok_rows = state.shape[2]
    feat_width = state.shape[3]
    head_dim = weights.shape[3] // 2
    head_count = feat_width // head_dim
    group_size = math.gcd(head_count, 4)
    group_count = head_count // group_size
    span_count = weights.shape[0]
    section_count = lax.axis_size("pipe")
    seq_total = tok_rows * lax.axis_size("ctx")
    score_scale = 1.0 / math.sqrt(head_dim)
    all_positions = token_positions(block_order, seq_total)
    own_positions = lax.dynamic_slice_in_dim(
        all_positions, lax.axis_index("ctx") * tok_rows, tok_rows
    )
    causal = all_positions[None, :] <= own_positions[:, None]
    section_index = lax.axis_index("pipe")
    carried = state[0, 0]
    start_column = start_span[:, 0]
    weight_grads = jnp.zeros((span_count, feat_width, 2 * head_dim), jnp.float32)
    for tick_index in range(out_grad.shape[0]):
        anchor = (section_index - tick_index) % section_count
        first_span = jnp.sum(
            jnp.where(jnp.arange(section_count, dtype=jnp.int32) == anchor, start_column, 0)
        )
        span_index = (first_span + (anchor + tick_index) // section_count) % 2
        weight = lax.dynamic_index_in_dim(weights[:, 0], span_index, 0, keepdims=False)
        widened = carried.astype(jnp.float32)
        normed = (widened * rms_scale(widened)).astype(jnp.bfloat16)
        split_heads = widened.reshape(tok_rows, head_count, head_dim)
        queries = (split_heads * rms_scale(split_heads)).astype(jnp.bfloat16)
        projected = jnp.dot(normed, weight, preferred_element_type=jnp.float32)
        key_raw = projected[:, :head_dim]
        key_scale = rms_scale(key_raw)
        key_unit = key_raw * key_scale
        own_rows = jnp.concatenate([key_unit, projected[:, head_dim:]], axis=1).astype(jnp.bfloat16)
        gathered = lax.all_gather(own_rows, "ctx", axis=0, tiled=True)
        key_rows = gathered[:, :head_dim]
        value_rows = gathered[:, head_dim:]
        query_groups = queries.reshape(tok_rows, group_count, group_size, head_dim).transpose(
            1, 0, 2, 3
        )

        def forward_group(query_part):
            scores = (
                jnp.einsum("qhd,kd->hqk", query_part, key_rows, preferred_element_type=jnp.float32)
                * score_scale
            )
            exponent = jnp.where(causal[None], jnp.exp(scores), 0.0)
            total_weight = jnp.sum(exponent, axis=-1, keepdims=True)
            probs = (exponent / total_weight).astype(jnp.bfloat16)
            attended = jnp.einsum(
                "hqk,kd->qhd", probs, value_rows, preferred_element_type=jnp.float32
            )
            return (probs, attended)

        probs, attended = lax.map(forward_group, query_groups)
        output = attended.transpose(1, 0, 2, 3).reshape(tok_rows, feat_width)
        updated = (widened + output * rms_scale(output)).astype(jnp.bfloat16)
        carried = from_behind(updated, "pipe", 1)
        upstream = out_grad[tick_index, 0, 0]
        upstream_groups = upstream.reshape(tok_rows, group_count, group_size, head_dim).transpose(
            1, 0, 2, 3
        )
        row_delta = jnp.sum(upstream_groups.astype(jnp.float32) * attended, axis=-1).transpose(
            0, 2, 1
        )
        key_grad = jnp.zeros((tok_rows * lax.axis_size("ctx"), head_dim), jnp.float32)
        value_grad = jnp.zeros((tok_rows * lax.axis_size("ctx"), head_dim), jnp.float32)
        for head_block in range(group_count):
            prob_part = probs[head_block]
            value_grad = value_grad + jnp.einsum(
                "hqk,qhd->kd",
                prob_part,
                upstream_groups[head_block],
                preferred_element_type=jnp.float32,
            )
            prob_grad = jnp.einsum(
                "qhd,kd->hqk",
                upstream_groups[head_block],
                value_rows,
                preferred_element_type=jnp.float32,
            )
            score_grad = (
                prob_part.astype(jnp.float32)
                * (prob_grad - row_delta[head_block][..., None])
                * score_scale
            ).astype(jnp.bfloat16)
            key_grad = key_grad + jnp.einsum(
                "hqk,qhd->kd",
                score_grad,
                query_groups[head_block],
                preferred_element_type=jnp.float32,
            )
        key_sums = lax.psum_scatter(
            jnp.concatenate([key_grad, value_grad], axis=1).astype(jnp.bfloat16),
            "ctx",
            scatter_dimension=0,
            tiled=True,
        ).astype(jnp.float32)
        key_delta = key_sums[:, :head_dim]
        key_back = key_scale * (
            key_delta - key_unit * jnp.mean(key_delta * key_unit, axis=-1, keepdims=True)
        )
        grad_rows = jnp.concatenate([key_back, key_sums[:, head_dim:]], axis=1).astype(jnp.bfloat16)
        local_grad = lax.dot_general(
            normed, grad_rows, (((0,), (0,)), ((), ())), preferred_element_type=jnp.float32
        )
        span_mask = (jnp.arange(span_count, dtype=jnp.int32) == span_index).astype(jnp.float32)[
            :, None, None
        ]
        masked_grad = span_mask * local_grad
        weight_grads = weight_grads + masked_grad
    weight_grads = lax.psum(weight_grads, ("ctx", "dp"))
    return (carried[None, None], weight_grads[:, None])


def solution(mesh):
    return jax.shard_map(
        shards,
        mesh=mesh,
        in_specs=(
            P("pipe", "dp", "ctx", None),
            P(None, "pipe", None, None),
            P(None, "pipe", "dp", "ctx", None),
            P(None, "dp"),
            P(),
        ),
        out_specs=(P("pipe", "dp", "ctx", None), P(None, "pipe", None, None)),
        check_vma=False,
    )
```

profile of v0, /device:TPU:16, one launch (start us, length us, event | category | flops | bytes accessed | tf_op | source)
XLA Modules:
  0.0 990.2 jit_solution(8186478735265335391)
XLA Ops:
  7.3 1.4 fusion.99
  10.5 1.2 fusion.58
  16.2 74.4 %all-gather.3.cloned.1.call-done = bf16[2048,256]{1,0:T(8,128)(2,1)} async-done(((bf16[128,256]{1,0:T(8,128)(2,1)}), bf16[2048,256]{1,0:T(8,128)(2,1)}) %all-gather.3.cloned.1.call-update) | async-done | bytes 1048592 | tf_op jit(solution)/shard_map/all_gather | solution.py:65
  90.6 1.3 fusion.117
  92.7 2.5 broadcast.232.clone2
  95.2 22.0 %while.26 = (s32[]{:T(128)}, bf16[2,4,128,2048]{2,3,1,0:T(8,128)(2,1)}, f32[2,128,4,128]{3,1,2,0:T(8,128)}, bf16[2,128,4,128]{1,3,2,0:T(8,128)(2,1)}, bf16[2048,...) while((s32[]{:T(128)}, ...), condition=%wide.region_7.8_spmd.clone, body=%wide.region_5.7_spmd.clone.sunk | while | flops 548666880 | bytes 33962720 | solution.py:85
  95.4 2.3 bitcast_reduce_fusion.4
  97.8 1.8 fusion.136
  100.5 2.5 copy.225
  103.0 3.2 constant_dynamic-update-slice_fusion.4
  106.4 2.3 bitcast_reduce_fusion.4
  108.8 1.8 fusion.136
  111.5 2.5 copy.225
  114.0 3.1 constant_dynamic-update-slice_fusion.4
  118.4 1.4 copy.152
  120.1 1.9 collective-permute-start
  122.8 6.8 collective-permute-done
  132.6 1.3 multiply_reduce_fusion.1
  134.4 2.3 convolution_bitcast_fusion.6
  136.7 2.3 fusion.38
  139.0 4.0 convolution_bitcast_fusion.8
  143.1 3.4 fusion.39
  149.1 56.5 %all-gather.5.cloned.1.call-done = bf16[2048,256]{1,0:T(8,128)(2,1)} async-done(((bf16[128,256]{1,0:T(8,128)(2,1)}), bf16[2048,256]{1,0:T(8,128)(2,1)}) %all-gather.5.cloned.1.call-update) | async-done | bytes 1048592 | tf_op jit(solution)/shard_map/all_gather | solution.py:65
  205.6 1.3 fusion.116
  207.7 2.5 broadcast.232.clone
  210.1 22.0 %while.27 = (s32[]{:T(128)}, bf16[2,4,128,2048]{2,3,1,0:T(8,128)(2,1)}, f32[2,128,4,128]{3,1,2,0:T(8,128)}, bf16[2,128,4,128]{1,3,2,0:T(8,128)(2,1)}, bf16[2048,...) while((s32[]{:T(128)}, ...), condition=%wide.region_15.16_spmd.clone, body=%wide.region_13.15_spmd.clone.sunk | while | flops 548666880 | bytes 33962720 | solution.py:85
  210.4 2.3 bitcast_reduce_fusion.5
  212.7 1.8 fusion.140
  215.5 2.5 copy.226
  218.0 3.2 constant_dynamic-update-slice_fusion.5
  221.4 2.3 bitcast_reduce_fusion.5
  223.7 1.8 fusion.140
  226.5 2.5 copy.226
  229.0 3.1 constant_dynamic-update-slice_fusion.5
  232.1 1.4 multiply_reduce_fusion
  233.6 2.3 convolution_bitcast_fusion.2
  235.9 2.3 fusion.36
  238.2 3.9 convolution_bitcast_fusion.4
  242.1 4.0 fusion.37
  246.2 2.2 pad_maximum_fusion.1
  248.4 35.8 %reduce-scatter.3.cloned.1.call-done = bf16[128,256]{1,0:T(8,128)(2,1)} async-done(((bf16[2048,256]{1,0:T(8,128)(2,1)}), bf16[128,256]{1,0:T(8,128)(2,1)}) %reduce-scatter.3.cloned.1.call-update) | async-done | bytes 65552 | tf_op jit(solution)/shard_map/reduce_scatter | solution.py:123
  287.2 73.8 %reduce-scatter.5.cloned.1.call-done = bf16[128,256]{1,0:T(8,128)(2,1)} async-done(((bf16[2048,256]{1,0:T(8,128)(2,1)}), bf16[128,256]{1,0:T(8,128)(2,1)}) %reduce-scatter.5.cloned.1.call-update) | async-done | bytes 65552 | tf_op jit(solution)/shard_map/reduce_scatter | solution.py:123
  363.9 1.7 add_bitcast_fusion
  365.6 1.4 copy.156
  368.5 1.9 collective-permute-start.1
  370.5 7.2 collective-permute-done.1
  377.7 602.2 %all-reduce.2.cloned.1.call-done = f32[2,1,1024,256]{3,2,1,0:T(8,128)} async-done(((f32[2,1,1024,256]{3,2,1,0:T(8,128)}), f32[2,1,1024,256]{3,2,1,0:T(8,128)}) %all-reduce.2.cloned.1.call-update) | async-done | bytes 2097168 | tf_op jit(solution)/shard_map/psum | solution.py:142
  980.6 3.0 copy.256
  (144 shorter events, 27.6 us)
Async XLA Ops:
  7.2 3.3 copy-start
  7.2 8.0 copy-start.23
  7.2 83.4 %all-gather.3.cloned.1.call-start = ((), (), s32[]{:S(2)}) async-start(), calls=%async_computation.2 | async-start | bytes 1114112 | tf_op jit(solution)/shard_map/all_gather | solution.py:65
  10.5 1.4 copy-start.19
  12.6 192.9 %all-gather.5.cloned.1.call-start = ((), (), s32[]{:S(2)}) async-start(), calls=%async_computation.3 | async-start | bytes 1114112 | tf_op jit(solution)/shard_map/all_gather | solution.py:65
  95.2 24.8 %copy-start.1 = (bf16[1,1,128,1024]{3,2,1,0:T(8,128)(2,1)S(1)}, bf16[1,1,128,1024]{3,2,1,0:T(8,128)(2,1)}, u32[]{:S(2)}) copy-start(bf16[1,1,128,1024]{3,2,1,0:T(8,128)(2,1)} %param.9) | copy-start | bytes 786436
  95.2 2.6 copy-start.13
  95.2 2.6 copy-start.15
  103.0 3.2 copy-start.14
  103.0 3.2 copy-start.16
  106.2 2.6 copy-start.13
  106.2 2.6 copy-start.15
  114.0 3.1 copy-start.14
  114.0 3.1 copy-start.16
  117.1 14.0 %copy-start.8 = (bf16[2,1,1,128,1024]{4,3,2,1,0:T(8,128)(2,1)S(1)}, bf16[2,1,1,128,1024]{4,3,2,1,0:T(8,128)(2,1)}, u32[]{:S(2)}) copy-start(bf16[2,1,1,128,1024]{4,3,2,1,0:T(8,128)(2,1)} %param.11) | copy-start | bytes 1572868
  120.1 9.4 collective-permute-start
  129.6 18.6 %copy-start.2 = (bf16[128,1024]{1,0:T(8,128)(2,1)}, bf16[128,1024]{1,0:T(8,128)(2,1)S(1)}, u32[]{:S(2)}) copy-start(bf16[128,1024]{1,0:T(8,128)(2,1)S(1)} %collective-permute-done) | copy-start | bytes 786436
  129.7 0.6 copy-start.21
  130.0 4.4 copy-start.5
  130.3 0.9 copy-start.17
  131.1 153.1 %reduce-scatter.3.cloned.1.call-start = ((), (), s32[]{:S(2)}) async-start(), calls=%async_computation.4 | async-start | bytes 1114112 | tf_op jit(solution)/shard_map/reduce_scatter | solution.py:123
  147.6 213.4 %reduce-scatter.5.cloned.1.call-start = ((), (), s32[]{:S(2)}) async-start(), calls=%async_computation.5 | async-start | bytes 1114112 | tf_op jit(solution)/shard_map/reduce_scatter | solution.py:123
  210.1 2.6 copy-start.9
  210.1 2.6 copy-start.11
  218.0 3.2 copy-start.10
  218.0 3.2 copy-start.12
  221.2 2.6 copy-start.9
  221.2 2.6 copy-start.11
  229.0 3.1 copy-start.10
  229.0 3.1 copy-start.12
  232.1 3.8 copy-start.4
  232.1 6.1 copy-start.7
  242.1 44.6 %copy-start.20 = (f32[128]{0:T(128)S(1)}, f32[128]{0:T(128)}, u32[]{:S(2)}) copy-start(f32[128]{0:T(128)} %copy-done.19) | copy-start | bytes 1540
  246.1 114.8 %copy-start.6 = (f32[128,256]{1,0:T(8,128)S(1)}, f32[128,256]{1,0:T(8,128)}, u32[]{:S(2)}) copy-start(f32[128,256]{1,0:T(8,128)} %copy-done.5) | copy-start | bytes 393220
  246.1 114.8 %copy-start.18 = (f32[128]{0:T(128)S(1)}, f32[128]{0:T(128)}, u32[]{:S(2)}) copy-start(f32[128]{0:T(128)} %copy-done.17) | copy-start | bytes 1540
  246.1 117.4 %copy-start.3 = (bf16[128,1024]{1,0:T(8,128)(2,1)S(1)}, bf16[128,1024]{1,0:T(8,128)(2,1)}, u32[]{:S(2)}) copy-start(bf16[128,1024]{1,0:T(8,128)(2,1)} %copy-done.2) | copy-start | bytes 786436
  246.1 117.4 %copy-start.22 = (f32[128]{0:T(128)S(1)}, f32[128]{0:T(128)}, u32[]{:S(2)}) copy-start(f32[128]{0:T(128)} %copy-done.21) | copy-start | bytes 1540
  248.4 731.6 %all-reduce.2.cloned.1.call-start = ((), (), s32[]{:S(2)}) async-start(), calls=%async_computation.6 | async-start | bytes 4194304 | tf_op jit(solution)/shard_map/psum | solution.py:142
  368.5 9.2 collective-permute-start.1
Sparse Core Ops, SparseCore 0:
  12.8 77.7 all-gather.2
  131.2 74.3 all-gather.4
  208.4 75.7 reduce-scatter.2
  287.7 73.2 reduce-scatter.4
  365.7 614.1 all-reduce.1
where the time goes:
time: 992 us; the launch traced here: 990 us
  waiting for transfers between devices  857 us (86%)
  local copies, waits for them, and re-layouts  44.1 us (4%)
  matrix products  43.5 us (4%)
  other arithmetic  25.8 us (3%)
  between operations  15.7 us (2%)
    psum x1, waiting for transfers between devices, shards(): weight_grads = lax.psum(weight_grads, ('ctx', 'dp'))  602 us
    all_gather x2, waiting for transfers between devices, shards(): gathered = lax.all_gather(own_rows, 'ctx', axis=0, tiled=True)  131 us
    reduce_scatter x2, waiting for transfers between devices, shards(): lax.psum_scatter(jnp.concatenate([key_grad, value_grad], axis=1).astype(j...  110 us
    dynamic_update_slice x8, local copies, waits for them, and re-layouts, shards(): probs, attended = lax.map(forward_group, query_groups)  22.5 us
  transfers between devices with their start and end apart: 7, of which 7 were waited for; matrix products, arithmetic and copies ran while one was open for 7% of the time, Pallas kernels for 0%

commit v1 on v0

--- a/solution.py
+++ b/solution.py
@@ -139,7 +139,7 @@
         ]
         masked_grad = span_mask * local_grad
         weight_grads = weight_grads + masked_grad
-    weight_grads = lax.psum(weight_grads, ("ctx", "dp"))
+    weight_grads = lax.psum(lax.psum(weight_grads, "dp"), "ctx")
     return (carried[None, None], weight_grads[:, None])
 
 

time: 992 us -> 606 us (0.61)
  the two profiles are of different devices: /device:TPU:16 before, /device:TPU:2 now
where the time goes in v1:
time: 606 us; the launch traced here: 605 us
  waiting for transfers between devices  471 us (78%)
  local copies, waits for them, and re-layouts  44.1 us (7%)
  matrix products  43.5 us (7%)
  other arithmetic  25.8 us (4%)
  between operations  16 us (3%)
    psum x2, waiting for transfers between devices, shards(): weight_grads = lax.psum(lax.psum(weight_grads, 'dp'), 'ctx')  215 us
    all_gather x2, waiting for transfers between devices, shards(): gathered = lax.all_gather(own_rows, 'ctx', axis=0, tiled=True)  130 us
    reduce_scatter x2, waiting for transfers between devices, shards(): lax.psum_scatter(jnp.concatenate([key_grad, value_grad], axis=1).astype(j...  109 us
    dynamic_update_slice x8, local copies, waits for them, and re-layouts, shards(): probs, attended = lax.map(forward_group, query_groups)  22.5 us
    ppermute x2, waiting for transfers between devices, from_behind(): return lax.ppermute(block, axis, route)  16.7 us
    dot_general x4, matrix products, shards(): jnp.einsum('hqk,qhd->kd', score_grad, query_groups[head_block], preferred...  15.3 us
  transfers between devices with their start and end apart: 8, of which 8 were waited for; matrix products, arithmetic and copies ran while one was open for 11% of the time, Pallas kernels for 0%

profile of v1, /device:TPU:2, one launch (start us, length us, event | category | flops | bytes accessed | tf_op | source)
XLA Modules:
  0.0 604.6 jit_solution(1136048243943000443)
XLA Ops:
  7.3 1.4 fusion.99
  16.2 74.6 %all-gather.3.cloned.1.call-done = bf16[2048,256]{1,0:T(8,128)(2,1)} async-done(((bf16[128,256]{1,0:T(8,128)(2,1)}), bf16[2048,256]{1,0:T(8,128)(2,1)}) %all-gather.3.cloned.1.call-update) | async-done | bytes 1048592 | tf_op jit(solution)/shard_map/all_gather | solution.py:65
  90.7 1.3 fusion.117
  92.9 2.5 broadcast.232.clone2
  95.3 22.0 %while.26 = (s32[]{:T(128)}, bf16[2,4,128,2048]{2,3,1,0:T(8,128)(2,1)}, f32[2,128,4,128]{3,1,2,0:T(8,128)}, bf16[2,128,4,128]{1,3,2,0:T(8,128)(2,1)}, bf16[2048,...) while((s32[]{:T(128)}, ...), condition=%wide.region_7.8_spmd.clone, body=%wide.region_5.7_spmd.clone.sunk | while | flops 548666880 | bytes 33962720 | solution.py:85
  95.6 2.3 bitcast_reduce_fusion.4
  97.9 1.8 fusion.136
  100.7 2.5 copy.225
  103.2 3.2 constant_dynamic-update-slice_fusion.4
  106.6 2.3 bitcast_reduce_fusion.4
  108.9 1.8 fusion.136
  111.7 2.5 copy.225
  114.2 3.1 constant_dynamic-update-slice_fusion.4
  118.5 1.4 copy.152
  120.3 1.9 collective-permute-start
  123.0 7.9 %collective-permute-done = bf16[128,1024]{1,0:T(8,128)(2,1)S(1)} collective-permute-done((bf16[128,1024]{1,0:T(8,128)(2,1)S(1)}, bf16[128,1024]{1,0:T(8,128)(2,1)S(1)}, u32[]{:S(2)}, u32[]{:S(2)}) %collective-permute-start) | collective-permute-done | bytes 262176 | tf_op jit(solution)/shard_map/ppermute | solution.py:13
  133.9 1.3 multiply_reduce_fusion.1
  135.7 2.3 convolution_bitcast_fusion.6
  138.0 2.3 fusion.38
  140.3 4.0 convolution_bitcast_fusion.8
  144.4 3.4 fusion.39
  150.4 55.4 %all-gather.5.cloned.1.call-done = bf16[2048,256]{1,0:T(8,128)(2,1)} async-done(((bf16[128,256]{1,0:T(8,128)(2,1)}), bf16[2048,256]{1,0:T(8,128)(2,1)}) %all-gather.5.cloned.1.call-update) | async-done | bytes 1048592 | tf_op jit(solution)/shard_map/all_gather | solution.py:65
  205.7 1.3 fusion.116
  207.8 2.5 broadcast.232.clone
  210.3 22.0 %while.27 = (s32[]{:T(128)}, bf16[2,4,128,2048]{2,3,1,0:T(8,128)(2,1)}, f32[2,128,4,128]{3,1,2,0:T(8,128)}, bf16[2,128,4,128]{1,3,2,0:T(8,128)(2,1)}, bf16[2048,...) while((s32[]{:T(128)}, ...), condition=%wide.region_15.16_spmd.clone, body=%wide.region_13.15_spmd.clone.sunk | while | flops 548666880 | bytes 33962720 | solution.py:85
  210.5 2.3 bitcast_reduce_fusion.5
  212.9 1.8 fusion.140
  215.6 2.5 copy.226
  218.1 3.2 constant_dynamic-update-slice_fusion.5
  221.5 2.3 bitcast_reduce_fusion.5
  223.9 1.8 fusion.140
  226.6 2.5 copy.226
  229.1 3.1 constant_dynamic-update-slice_fusion.5
  232.3 1.4 multiply_reduce_fusion
  233.7 2.3 convolution_bitcast_fusion.2
  236.0 2.3 fusion.36
  238.3 3.9 convolution_bitcast_fusion.4
  242.3 4.0 fusion.37
  246.3 2.2 pad_maximum_fusion.1
  248.6 36.1 %reduce-scatter.3.cloned.1.call-done = bf16[128,256]{1,0:T(8,128)(2,1)} async-done(((bf16[2048,256]{1,0:T(8,128)(2,1)}), bf16[128,256]{1,0:T(8,128)(2,1)}) %reduce-scatter.3.cloned.1.call-update) | async-done | bytes 65552 | tf_op jit(solution)/shard_map/reduce_scatter | solution.py:123
  287.6 73.4 %reduce-scatter.5.cloned.1.call-done = bf16[128,256]{1,0:T(8,128)(2,1)} async-done(((bf16[2048,256]{1,0:T(8,128)(2,1)}), bf16[128,256]{1,0:T(8,128)(2,1)}) %reduce-scatter.5.cloned.1.call-update) | async-done | bytes 65552 | tf_op jit(solution)/shard_map/reduce_scatter | solution.py:123
  364.0 1.7 multiply_add_fusion
  365.7 65.8 %all-reduce.3.cloned.1.call-done = f32[2,1024,256]{2,1,0:T(8,128)} async-done(((f32[2,1024,256]{2,1,0:T(8,128)}), f32[2,1024,256]{2,1,0:T(8,128)}) %all-reduce.3.cloned.1.call-update) | async-done | bytes 2097168 | tf_op jit(solution)/shard_map/psum | solution.py:142
  431.6 1.4 copy.156
  434.5 1.9 collective-permute-start.1
  436.4 8.8 %collective-permute-done.1 = bf16[128,1024]{1,0:T(8,128)(2,1)S(1)} collective-permute-done((bf16[128,1024]{1,0:T(8,128)(2,1)S(1)}, bf16[128,1024]{1,0:T(8,128)(2,1)S(1)}, u32[]{:S(2)}, u32[]{:S(2)}) %collective-permute-start.1) | collective-permute-done | bytes 262176 | tf_op jit(solution)/shard_map/ppermute | solution.py:13
  445.3 148.7 %all-reduce.5.cloned.1.call-done = f32[2,1,1024,256]{3,2,1,0:T(8,128)} async-done(((f32[2,1,1024,256]{3,2,1,0:T(8,128)}), f32[2,1,1024,256]{3,2,1,0:T(8,128)}) %all-reduce.5.cloned.1.call-update) | async-done | bytes 2097168 | tf_op jit(solution)/shard_map/psum | solution.py:142
  594.7 3.0 copy.257
  (147 shorter events, 28.9 us)
Async XLA Ops:
  7.2 3.3 copy-start
  7.2 8.0 %copy-start.23 = (s32[32]{0:T(128)S(1)}, s32[32]{0:T(128)}, u32[]{:S(2)}) copy-start(s32[32]{0:T(128)} %param.13) | copy-start | bytes 388
  7.2 83.6 %all-gather.3.cloned.1.call-start = ((), (), s32[]{:S(2)}) async-start(), calls=%async_computation.2 | async-start | bytes 1114112 | tf_op jit(solution)/shard_map/all_gather | solution.py:65
  10.5 1.4 copy-start.19
  12.6 193.1 %all-gather.5.cloned.1.call-start = ((), (), s32[]{:S(2)}) async-start(), calls=%async_computation.3 | async-start | bytes 1114112 | tf_op jit(solution)/shard_map/all_gather | solution.py:65
  95.3 24.8 %copy-start.1 = (bf16[1,1,128,1024]{3,2,1,0:T(8,128)(2,1)S(1)}, bf16[1,1,128,1024]{3,2,1,0:T(8,128)(2,1)}, u32[]{:S(2)}) copy-start(bf16[1,1,128,1024]{3,2,1,0:T(8,128)(2,1)} %param.9) | copy-start | bytes 786436
  95.3 2.6 copy-start.13
  95.3 2.6 copy-start.15
  103.2 3.2 copy-start.14
  103.2 3.2 copy-start.16
  106.3 2.6 copy-start.13
  106.3 2.6 copy-start.15
  114.2 3.1 copy-start.14
  114.2 3.1 copy-start.16
  117.3 15.1 %copy-start.8 = (bf16[2,1,1,128,1024]{4,3,2,1,0:T(8,128)(2,1)S(1)}, bf16[2,1,1,128,1024]{4,3,2,1,0:T(8,128)(2,1)}, u32[]{:S(2)}) copy-start(bf16[2,1,1,128,1024]{4,3,2,1,0:T(8,128)(2,1)} %param.11) | copy-start | bytes 1572868
  120.3 10.6 %collective-permute-start = (bf16[128,1024]{1,0:T(8,128)(2,1)S(1)}, bf16[128,1024]{1,0:T(8,128)(2,1)S(1)}, u32[]{:S(2)}, u32[]{:S(2)}) collective-permute-start(bf16[128,1024]{1,0:T(8,128)(2,1)S(1)} %fusion.63), channel_id=1, source_target_pairs={{448,0},{0,64},{64,128},{128,192},{192,256},{256,320},{320,384},{3... | collective-permute-start | bytes 786440 | tf_op jit(solution)/shard_map/ppermute | solution.py:13
  130.8 18.6 %copy-start.2 = (bf16[128,1024]{1,0:T(8,128)(2,1)}, bf16[128,1024]{1,0:T(8,128)(2,1)S(1)}, u32[]{:S(2)}) copy-start(bf16[128,1024]{1,0:T(8,128)(2,1)S(1)} %collective-permute-done) | copy-start | bytes 786436
  131.0 0.6 copy-start.21
  131.3 4.4 copy-start.5
  131.6 0.9 copy-start.17
  132.3 152.3 %reduce-scatter.3.cloned.1.call-start = ((), (), s32[]{:S(2)}) async-start(), calls=%async_computation.4 | async-start | bytes 1114112 | tf_op jit(solution)/shard_map/reduce_scatter | solution.py:123
  148.8 212.1 %reduce-scatter.5.cloned.1.call-start = ((), (), s32[]{:S(2)}) async-start(), calls=%async_computation.5 | async-start | bytes 1114112 | tf_op jit(solution)/shard_map/reduce_scatter | solution.py:123
  210.3 2.6 copy-start.9
  210.3 2.6 copy-start.11
  218.1 3.2 copy-start.10
  218.1 3.2 copy-start.12
  221.3 2.6 copy-start.9
  221.3 2.6 copy-start.11
  229.1 3.1 copy-start.10
  229.1 3.1 copy-start.12
  232.3 3.8 copy-start.4
  232.3 6.1 %copy-start.7 = (bf16[2048,256]{1,0:T(8,128)(2,1)S(1)}, bf16[2048,256]{1,0:T(8,128)(2,1)}, u32[]{:S(2)}) copy-start(bf16[2048,256]{1,0:T(8,128)(2,1)} %all-gather.5.cloned.1.call-done) | copy-start | bytes 3145732
  242.3 44.9 %copy-start.20 = (f32[128]{0:T(128)S(1)}, f32[128]{0:T(128)}, u32[]{:S(2)}) copy-start(f32[128]{0:T(128)} %copy-done.19) | copy-start | bytes 1540
  246.3 114.7 %copy-start.6 = (f32[128,256]{1,0:T(8,128)S(1)}, f32[128,256]{1,0:T(8,128)}, u32[]{:S(2)}) copy-start(f32[128,256]{1,0:T(8,128)} %copy-done.5) | copy-start | bytes 393220
  246.3 114.7 %copy-start.18 = (f32[128]{0:T(128)S(1)}, f32[128]{0:T(128)}, u32[]{:S(2)}) copy-start(f32[128]{0:T(128)} %copy-done.17) | copy-start | bytes 1540
  246.3 117.3 %copy-start.3 = (bf16[128,1024]{1,0:T(8,128)(2,1)S(1)}, bf16[128,1024]{1,0:T(8,128)(2,1)}, u32[]{:S(2)}) copy-start(bf16[128,1024]{1,0:T(8,128)(2,1)} %copy-done.2) | copy-start | bytes 786436
  246.3 117.3 %copy-start.22 = (f32[128]{0:T(128)S(1)}, f32[128]{0:T(128)}, u32[]{:S(2)}) copy-start(f32[128]{0:T(128)} %copy-done.21) | copy-start | bytes 1540
  248.5 183.0 %all-reduce.3.cloned.1.call-start = ((), (), s32[]{:S(2)}) async-start(), calls=%async_computation.6 | async-start | bytes 4194304 | tf_op jit(solution)/shard_map/psum | solution.py:142
  365.6 228.4 %all-reduce.5.cloned.1.call-start = ((), (), s32[]{:S(2)}) async-start(), calls=%async_computation.7 | async-start | bytes 4194304 | tf_op jit(solution)/shard_map/psum | solution.py:142
  434.5 10.8 %collective-permute-start.1 = (bf16[128,1024]{1,0:T(8,128)(2,1)S(1)}, bf16[128,1024]{1,0:T(8,128)(2,1)S(1)}, u32[]{:S(2)}, u32[]{:S(2)}) collective-permute-start(bf16[128,1024]{1,0:T(8,128)(2,1)S(1)} %add_convert_fusion), channel_id=1, source_target_pairs={{448,0},{0,64},{64,128},{128,192},{192,256},{256,320},{320,384},{3... | collective-permute-start | bytes 786440 | tf_op jit(solution)/shard_map/ppermute | solution.py:13
Sparse Core Ops, SparseCore 0:
  12.8 77.9 all-gather.2
  132.5 73.2 all-gather.4
  208.5 76.0 reduce-scatter.2
  288.1 72.8 reduce-scatter.4
  365.8 65.7 all-reduce.2
  434.6 159.3 all-reduce.4
